TPU v7x, 32 devices: a whole 2x2x4 slice. The times are simulated.
32 devices in a mesh: groups: 2 (over y), row: 4 (over z), col: 4 (over x, core).
Axes of the slice: x: 2, y: 2, z: 4, core: 2. Of those that a mesh axis runs over, the one named last changes fastest.
Arguments:
- factor_blocks: bfloat16 [20, 4096, 4096], P('groups', 'row', 'col'), parts along dimension 0, may hold values from -0.0390625 to 0.0390625
- inverse_blocks: bfloat16 [10, 4096, 4096], P('groups', 'col', 'row'), parts along dimension 0, as said below
- right_sides: bfloat16 [10, 4096, 256], P('groups', 'row'), parts along dimension 0, may hold values from -6 to 6
Outputs:
- solution: bfloat16 [10, 4096, 256], P('groups', 'col', 'row'), parts along dimension 0
There are 2 independent parts, one for each index of `groups`. A program takes and returns all parts, laid end to end along the dimension named above; each array names one. Nothing has to cross between parts.
Inputs may be any that keep to these rules, and one draw needn't show every extreme that they name: `inverse_blocks`: each block is lower triangular with a diagonal of 0.5 to 2, hence invertible.
All inputs are finite; a program needn't handle non-finite values.
Results may differ from a plain program's by a relative error of at most 0.0095.
Values may be sent and summed in bfloat16 or wider, within the bound.
A program may use at most 64 MiB of HBM per device.

v0:
```python
import jax
import jax.numpy as jnp
from jax import lax
from jax.sharding import PartitionSpec as P


def pair_index(block_row, column_index):
    return block_row * (block_row - 1) // 2 + column_index


def per_device(factor_blocks, inverse_blocks, right_sides):
    steps_total = right_sides.shape[0]
    angles = right_sides.shape[2]
    col_rows = inverse_blocks.shape[1]
    solved = []
    outputs = []
    for block_row in range(steps_total):
        residual = right_sides[block_row].astype(jnp.float32)
        if block_row > 0:
            partial_value = jnp.zeros((right_sides.shape[1], angles), jnp.float32)
            for column_index in range(block_row):
                partial_value = partial_value + jnp.dot(
                    factor_blocks[pair_index(block_row, column_index)],
                    solved[column_index],
                    preferred_element_type=jnp.float32,
                )
            residual = residual - lax.psum(partial_value, "col")
        residual_bf = residual.astype(jnp.bfloat16)
        term = jnp.dot(inverse_blocks[block_row], residual_bf, preferred_element_type=jnp.float32)
        share = lax.psum_scatter(term, "row", scatter_dimension=1, tiled=True).astype(jnp.bfloat16)
        outputs.append(share)
        if block_row + 1 < steps_total:
            current = lax.all_gather(share, "row", axis=1, tiled=True)
        else:
            current = jnp.zeros((col_rows, angles), jnp.bfloat16)
        solved.append(current)
    return jnp.stack(outputs, axis=0)


def solution(mesh):
    placed = (P("groups", "row", "col"), P("groups", "col", "row"), P("groups", "row", None))
    return jax.shard_map(
        per_device, mesh=mesh, in_specs=placed, out_specs=P("groups", "col", "row"), check_vma=False
    )
```

profile of v0, /device:TPU:0, one launch (start us, length us, event | category | flops | bytes accessed | tf_op | source)
XLA Modules:
  0.0 406.6 jit_solution(15479284260959443623)
XLA Ops:
  6.5 3.4 fusion.28
  9.9 0.0 reduce-scatter.6.cloned.1.call-update
  10.0 0.0 all-reduce.5.cloned.1.call-start
  10.0 30.1 %reduce-scatter.6.cloned.1.call-done = f32[1024,64]{0,1:T(8,128)} async-done(((f32[1024,256]{0,1:T(8,128)}), f32[1024,64]{0,1:T(8,128)}) %reduce-scatter.6.cloned.1.call-update) | async-done | bytes 262160 | tf_op jit(solution)/shard_map/reduce_scatter | solution.py:30
  40.1 1.6 bitcast_dynamic-update-slice_fusion.4
  41.8 15.9 %all_gather.12 = bf16[1024,256]{0,1:T(8,128)(2,1)S(1)} all-gather(bf16[1024,64]{0,1:T(8,128)(2,1)S(1)} %get-tuple-element.12), channel_id=1, replica_groups=mesh['groups'=2,'row'=4,'col'=4] {'row'}, dimensions={1}, use_global_device_ids=true | all-gather | bytes 655360 | tf_op jit(solution)/shard_map/all_gather | solution.py:33
  57.7 3.5 fusion.45
  61.2 0.0 all-reduce.5.cloned.1.call-update
  61.2 0.0 reduce-scatter.8.cloned.1.call-start
  61.3 34.7 %all-reduce.5.cloned.1.call-done = f32[1024,256]{1,0:T(8,128)} async-done(((f32[1024,256]{1,0:T(8,128)}), f32[1024,256]{1,0:T(8,128)}) %all-reduce.5.cloned.1.call-update) | async-done | bytes 1048592 | tf_op jit(solution)/shard_map/psum | solution.py:27
  96.0 3.7 fusion.48
  99.7 0.0 reduce-scatter.8.cloned.1.call-update
  99.7 0.0 all-reduce.7.cloned.1.call-start
  99.8 27.9 %reduce-scatter.8.cloned.1.call-done = f32[1024,64]{0,1:T(8,128)} async-done(((f32[1024,256]{0,1:T(8,128)}), f32[1024,64]{0,1:T(8,128)}) %reduce-scatter.8.cloned.1.call-update) | async-done | bytes 262160 | tf_op jit(solution)/shard_map/reduce_scatter | solution.py:30
  127.6 1.6 bitcast_dynamic-update-slice_fusion.3
  129.3 16.0 %all_gather.13 = bf16[1024,256]{0,1:T(8,128)(2,1)S(1)} all-gather(bf16[1024,64]{0,1:T(8,128)(2,1)S(1)} %get-tuple-element.10), channel_id=1, replica_groups=mesh['groups'=2,'row'=4,'col'=4] {'row'}, dimensions={1}, use_global_device_ids=true | all-gather | bytes 655360 | tf_op jit(solution)/shard_map/all_gather | solution.py:33
  145.2 0.8 copy-done.4
  146.0 2.3 fusion.20
  148.4 3.3 fusion.63
  151.7 0.0 all-reduce.7.cloned.1.call-update
  151.7 0.0 reduce-scatter.10.cloned.1.call-start
  151.8 34.7 %all-reduce.7.cloned.1.call-done = f32[1024,256]{1,0:T(8,128)} async-done(((f32[1024,256]{1,0:T(8,128)}), f32[1024,256]{1,0:T(8,128)}) %all-reduce.7.cloned.1.call-update) | async-done | bytes 1048592 | tf_op jit(solution)/shard_map/psum | solution.py:27
  186.5 3.6 fusion.51
  190.1 0.0 reduce-scatter.10.cloned.1.call-update
  190.1 0.0 all-reduce.9.cloned.1.call-start
  190.2 3.5 fusion.14
  193.7 24.4 %reduce-scatter.10.cloned.1.call-done = f32[1024,64]{0,1:T(8,128)} async-done(((f32[1024,256]{0,1:T(8,128)}), f32[1024,64]{0,1:T(8,128)}) %reduce-scatter.10.cloned.1.call-update) | async-done | bytes 262160 | tf_op jit(solution)/shard_map/reduce_scatter | solution.py:30
  218.0 1.7 bitcast_dynamic-update-slice_fusion.2
  219.8 16.0 %all_gather.14 = bf16[1024,256]{0,1:T(8,128)(2,1)S(1)} all-gather(bf16[1024,64]{0,1:T(8,128)(2,1)S(1)} %get-tuple-element.8), channel_id=1, replica_groups=mesh['groups'=2,'row'=4,'col'=4] {'row'}, dimensions={1}, use_global_device_ids=true | all-gather | bytes 655360 | tf_op jit(solution)/shard_map/all_gather | solution.py:33
  235.7 0.8 copy-done.5
  236.5 2.3 fusion.12
  238.9 3.3 fusion.72
  242.2 0.0 reduce-scatter.12.cloned.1.call-start
  242.3 34.7 %all-reduce.9.cloned.1.call-done = f32[1024,256]{1,0:T(8,128)} async-done(((f32[1024,256]{1,0:T(8,128)}), f32[1024,256]{1,0:T(8,128)}) %all-reduce.9.cloned.1.call-update) | async-done | bytes 1048592 | tf_op jit(solution)/shard_map/psum | solution.py:27
  277.0 3.6 fusion.54
  280.6 0.0 all-reduce.11.cloned.1.call-start
  280.7 3.6 fusion.6
  284.3 3.3 fusion.4
  287.6 21.0 %reduce-scatter.12.cloned.1.call-done = f32[1024,64]{0,1:T(8,128)} async-done(((f32[1024,256]{0,1:T(8,128)}), f32[1024,64]{0,1:T(8,128)}) %reduce-scatter.12.cloned.1.call-update) | async-done | bytes 262160 | tf_op jit(solution)/shard_map/reduce_scatter | solution.py:30
  308.6 1.8 bitcast_dynamic-update-slice_fusion.1
  310.3 15.9 %all_gather.15 = bf16[1024,256]{0,1:T(8,128)(2,1)S(1)} all-gather(bf16[1024,64]{0,1:T(8,128)(2,1)S(1)} %get-tuple-element.6), channel_id=1, replica_groups=mesh['groups'=2,'row'=4,'col'=4] {'row'}, dimensions={1}, use_global_device_ids=true | all-gather | bytes 655360 | tf_op jit(solution)/shard_map/all_gather | solution.py:33
  326.2 2.3 fusion.2
  328.6 3.4 fusion.84
  332.0 0.0 reduce-scatter.14.cloned.1.call-start
  332.1 34.8 %all-reduce.11.cloned.1.call-done = f32[1024,256]{1,0:T(8,128)} async-done(((f32[1024,256]{1,0:T(8,128)}), f32[1024,256]{1,0:T(8,128)}) %all-reduce.11.cloned.1.call-update) | async-done | bytes 1048592 | tf_op jit(solution)/shard_map/psum | solution.py:27
  366.8 3.7 fusion.57
  370.5 27.9 %reduce-scatter.14.cloned.1.call-done = f32[1024,64]{0,1:T(8,128)} async-done(((f32[1024,256]{0,1:T(8,128)}), f32[1024,64]{0,1:T(8,128)}) %reduce-scatter.14.cloned.1.call-update) | async-done | bytes 262160 | tf_op jit(solution)/shard_map/reduce_scatter | solution.py:30
  398.4 1.6 bitcast_dynamic-update-slice_fusion
  (17 shorter events, 0.1 us)
Async XLA Ops:
  6.5 33.6 %reduce-scatter.6.cloned.1.call-start = ((), (), s32[]{:S(2)}) async-start(), calls=%async_computation.5 | async-start | bytes 1310720 | tf_op jit(solution)/shard_map/reduce_scatter | solution.py:30
  10.0 86.0 %all-reduce.5.cloned.1.call-start = ((), (), s32[]{:S(2)}) async-start(), calls=%async_computation.6 | async-start | bytes 2097152 | tf_op jit(solution)/shard_map/psum | solution.py:27
  57.7 38.3 %copy-start = (bf16[5,1024,256]{2,1,0:T(8,128)(2,1)S(1)}, bf16[5,1024,256]{2,1,0:T(8,128)(2,1)}, u32[]{:S(2)}) copy-start(bf16[5,1024,256]{2,1,0:T(8,128)(2,1)} %param.5) | copy-start | bytes 7864324
  61.2 66.4 %reduce-scatter.8.cloned.1.call-start = ((), (), s32[]{:S(2)}) async-start(), calls=%async_computation.7 | async-start | bytes 1310720 | tf_op jit(solution)/shard_map/reduce_scatter | solution.py:30
  99.7 86.7 %all-reduce.7.cloned.1.call-start = ((), (), s32[]{:S(2)}) async-start(), calls=%async_computation.8 | async-start | bytes 2097152 | tf_op jit(solution)/shard_map/psum | solution.py:27
  145.2 0.8 copy-start.4
  151.7 66.3 %reduce-scatter.10.cloned.1.call-start = ((), (), s32[]{:S(2)}) async-start(), calls=%async_computation.9 | async-start | bytes 1310720 | tf_op jit(solution)/shard_map/reduce_scatter | solution.py:30
  190.1 86.8 %all-reduce.9.cloned.1.call-start = ((), (), s32[]{:S(2)}) async-start(), calls=%async_computation.10 | async-start | bytes 2097152 | tf_op jit(solution)/shard_map/psum | solution.py:27
  218.0 20.8 %copy-start.3 = (f32[256,1024]{0,1:T(8,128)S(1)}, f32[256,1024]{0,1:T(8,128)}, u32[]{:S(2)}) copy-start(f32[256,1024]{0,1:T(8,128)} %fusion.14) | copy-start | bytes 3145732
  235.7 0.8 copy-start.5
  242.2 66.3 %reduce-scatter.12.cloned.1.call-start = ((), (), s32[]{:S(2)}) async-start(), calls=%async_computation.11 | async-start | bytes 1310720 | tf_op jit(solution)/shard_map/reduce_scatter | solution.py:30
  280.6 86.2 %all-reduce.11.cloned.1.call-start = ((), (), s32[]{:S(2)}) async-start(), calls=%async_computation.12 | async-start | bytes 2097152 | tf_op jit(solution)/shard_map/psum | solution.py:27
  280.7 3.6 copy-start.6
  308.6 20.0 %copy-start.1 = (f32[256,1024]{0,1:T(8,128)S(1)}, f32[256,1024]{0,1:T(8,128)}, u32[]{:S(2)}) copy-start(f32[256,1024]{0,1:T(8,128)} %fusion.6) | copy-start | bytes 3145732
  308.6 20.0 %copy-start.2 = (f32[256,1024]{0,1:T(8,128)S(1)}, f32[256,1024]{0,1:T(8,128)}, u32[]{:S(2)}) copy-start(f32[256,1024]{0,1:T(8,128)} %fusion.4) | copy-start | bytes 3145732
  332.0 66.4 %reduce-scatter.14.cloned.1.call-start = ((), (), s32[]{:S(2)}) async-start(), calls=%async_computation.13 | async-start | bytes 1310720 | tf_op jit(solution)/shard_map/reduce_scatter | solution.py:30
Sparse Core Ops, SparseCore 0:
  10.1 29.9 reduce-scatter.5
  61.3 34.6 all-reduce.4
  99.8 27.7 reduce-scatter.7
  151.8 34.5 all-reduce.6
  190.2 27.7 reduce-scatter.9
  242.3 34.5 all-reduce.8
  280.8 27.7 reduce-scatter.11
  332.1 34.6 all-reduce.10
  370.6 27.7 reduce-scatter.13
where the time goes:
time: 407 us
  waiting for transfers between devices  270 us (66%)
  blocking collectives  63.8 us (16%)
  matrix products  49 us (12%)
  between operations  13.3 us (3%)
  other arithmetic  8.36 us (2%)
    psum x4, waiting for transfers between devices, per_device(): residual = residual - lax.psum(partial_value, 'col')  139 us
    reduce_scatter x5, waiting for transfers between devices, per_device(): lax.psum_scatter(term, 'row', scatter_dimension=1, tiled=True)  131 us
    all_gather x4, blocking collectives, per_device(): current = lax.all_gather(share, 'row', axis=1, tiled=True)  63.8 us
    dot_general x10, matrix products, per_device(): jnp.dot(factor_blocks[pair_index(block_row, column_index)], solved[column...  30.9 us
    dot_general x5, matrix products, per_device(): jnp.dot(inverse_blocks[block_row], residual_bf, preferred_element_type=jn...  18.1 us
  transfers between devices with their start and end apart: 9, of which 9 were waited for; matrix products, arithmetic and copies ran while one was open for 3% of the time, Pallas kernels for 0%

commit v1 on v0

--- a/solution.py
+++ b/solution.py
@@ -30,7 +30,18 @@
         share = lax.psum_scatter(term, "row", scatter_dimension=1, tiled=True).astype(jnp.bfloat16)
         outputs.append(share)
         if block_row + 1 < steps_total:
-            current = lax.all_gather(share, "row", axis=1, tiled=True)
+            ways, here, step = (lax.axis_size("row"), lax.axis_index("row"), share.shape[1])
+            line, have = (share, 1)
+            while have < ways:
+                line = jnp.concatenate(
+                    [
+                        line,
+                        lax.ppermute(line, "row", [(d, (d - have) % ways) for d in range(ways)]),
+                    ],
+                    axis=1,
+                )
+                have = 2 * have
+            current = jnp.roll(line, here * step, axis=1)
         else:
             current = jnp.zeros((col_rows, angles), jnp.bfloat16)
         solved.append(current)

time: 407 us -> 428 us (1.052)
  waiting for transfers between devices: 270 us -> 344 us
  blocking collectives: 63.8 us -> 0 us
  starting transfers between devices: 0.34 us -> 8.75 us
  other arithmetic: 8.36 us -> 12.7 us
    all_gather x4 -> x0, blocking collectives: 63.8 us -> none  [per_device(): current = lax.all_gather(share, 'row', axis=1, tiled=True)]
    ppermute x0 -> x8, waiting for transfers between devices: none -> 56.4 us  [per_device(): lax.ppermute(line, 'row', [(d, (d - have) % ways) for d in range(ways)])]
    reduce_scatter x5, waiting for transfers between devices: 131 us -> 142 us  [per_device(): lax.psum_scatter(term, 'row', scatter_dimension=1, tiled=True)]
    ppermute x0 -> x8, starting transfers between devices: none -> 8.41 us  [per_device(): lax.ppermute(line, 'row', [(d, (d - have) % ways) for d in range(ways)])]
    psum x4, waiting for transfers between devices: 139 us -> 146 us  [per_device(): residual = residual - lax.psum(partial_value, 'col')]
    concatenate x0 -> x7, other arithmetic: none -> 4.47 us  [the longest x3 4.4 us: per_device(): current = jnp.roll(line, here * step, axis=1)]
  transfers between devices with their start and end apart: 9 -> 17, of which waited for: 9 -> 17; matrix products, arithmetic and copies ran while one was open for 3% -> 2% of each run, Pallas kernels for 0% -> 0%
where the time goes in v1:
time: 428 us; the launch traced here: 427 us
  waiting for transfers between devices  344 us (80%)
  matrix products  46.6 us (11%)
  between operations  13.3 us (3%)
  other arithmetic  12.7 us (3%)
  starting transfers between devices  8.75 us (2%)
    psum x4, waiting for transfers between devices, per_device(): residual = residual - lax.psum(partial_value, 'col')  146 us
    reduce_scatter x5, waiting for transfers between devices, per_device(): lax.psum_scatter(term, 'row', scatter_dimension=1, tiled=True)  142 us
    ppermute x8, waiting for transfers between devices, per_device(): lax.ppermute(line, 'row', [(d, (d - have) % ways) for d in range(ways)])  56.4 us
    dot_general x10, matrix products, per_device(): jnp.dot(factor_blocks[pair_index(block_row, column_index)], solved[column...  28.5 us
    dot_general x5, matrix products, per_device(): jnp.dot(inverse_blocks[block_row], residual_bf, preferred_element_type=jn...  18.1 us
  transfers between devices with their start and end apart: 17, of which 17 were waited for; matrix products, arithmetic and copies ran while one was open for 2% of the time, Pallas kernels for 0%

profile of v1, /device:TPU:0, one launch (start us, length us, event | category | flops | bytes accessed | tf_op | source)
XLA Modules:
  0.0 427.4 jit_solution(18144580743646896256)
XLA Ops:
  6.5 3.4 fusion.28
  10.0 30.1 %reduce-scatter.6.cloned.1.call-done = f32[1024,64]{0,1:T(8,128)} async-done(((f32[1024,256]{0,1:T(8,128)}), f32[1024,64]{0,1:T(8,128)}) %reduce-scatter.6.cloned.1.call-update) | async-done | bytes 262160 | tf_op jit(solution)/shard_map/reduce_scatter | solution.py:30
  40.1 1.6 bitcast_dynamic-update-slice_fusion.4
  41.8 0.9 collective-permute-start
  42.7 4.1 collective-permute-done
  46.8 1.2 collective-permute-start.1
  48.0 11.9 %collective-permute-done.1 = bf16[1024,128]{0,1:T(8,128)(2,1)S(1)} collective-permute-done((bf16[1024,128]{0,1:T(8,128)(2,1)S(1)}, bf16[1024,128]{0,1:T(8,128)(2,1)S(1)}, u32[]{:S(2)}, u32[]{:S(2)}) %collective-permute-start.1) | collective-permute-done | bytes 262176 | tf_op jit(solution)/shard_map/ppermute | solution.py:39
  59.9 1.5 fusion.114
  61.3 3.5 fusion.45
  64.9 36.6 %all-reduce.5.cloned.1.call-done = f32[1024,256]{1,0:T(8,128)} async-done(((f32[1024,256]{1,0:T(8,128)}), f32[1024,256]{1,0:T(8,128)}) %all-reduce.5.cloned.1.call-update) | async-done | bytes 1048592 | tf_op jit(solution)/shard_map/psum | solution.py:27
  101.5 3.7 fusion.48
  105.2 27.9 %reduce-scatter.8.cloned.1.call-done = f32[1024,64]{0,1:T(8,128)} async-done(((f32[1024,256]{0,1:T(8,128)}), f32[1024,64]{0,1:T(8,128)}) %reduce-scatter.8.cloned.1.call-update) | async-done | bytes 262160 | tf_op jit(solution)/shard_map/reduce_scatter | solution.py:30
  133.1 1.6 bitcast_dynamic-update-slice_fusion.3
  134.7 0.9 collective-permute-start.2
  135.6 4.1 collective-permute-done.2
  139.7 1.2 collective-permute-start.3
  140.9 11.9 %collective-permute-done.3 = bf16[1024,128]{0,1:T(8,128)(2,1)S(1)} collective-permute-done((bf16[1024,128]{0,1:T(8,128)(2,1)S(1)}, bf16[1024,128]{0,1:T(8,128)(2,1)S(1)}, u32[]{:S(2)}, u32[]{:S(2)}) %collective-permute-start.3) | collective-permute-done | bytes 262176 | tf_op jit(solution)/shard_map/ppermute | solution.py:39
  152.8 1.5 fusion.109
  155.1 2.3 fusion.20
  157.4 3.3 fusion.63
  160.8 36.6 %all-reduce.7.cloned.1.call-done = f32[1024,256]{1,0:T(8,128)} async-done(((f32[1024,256]{1,0:T(8,128)}), f32[1024,256]{1,0:T(8,128)}) %all-reduce.7.cloned.1.call-update) | async-done | bytes 1048592 | tf_op jit(solution)/shard_map/psum | solution.py:27
  197.4 3.7 fusion.51
  201.1 27.9 %reduce-scatter.10.cloned.1.call-done = f32[1024,64]{0,1:T(8,128)} async-done(((f32[1024,256]{0,1:T(8,128)}), f32[1024,64]{0,1:T(8,128)}) %reduce-scatter.10.cloned.1.call-update) | async-done | bytes 262160 | tf_op jit(solution)/shard_map/reduce_scatter | solution.py:30
  229.0 1.6 bitcast_dynamic-update-slice_fusion.2
  230.6 0.9 collective-permute-start.4
  231.5 4.1 collective-permute-done.4
  235.6 1.2 collective-permute-start.5
  236.8 2.5 fusion.14
  239.3 9.4 %collective-permute-done.5 = bf16[1024,128]{0,1:T(8,128)(2,1)S(1)} collective-permute-done((bf16[1024,128]{0,1:T(8,128)(2,1)S(1)}, bf16[1024,128]{0,1:T(8,128)(2,1)S(1)}, u32[]{:S(2)}, u32[]{:S(2)}) %collective-permute-start.5) | collective-permute-done | bytes 262176 | tf_op jit(solution)/shard_map/ppermute | solution.py:39
  248.7 1.5 fusion.104
  251.0 2.3 fusion.12
  253.3 3.3 fusion.72
  256.7 36.6 %all-reduce.9.cloned.1.call-done = f32[1024,256]{1,0:T(8,128)} async-done(((f32[1024,256]{1,0:T(8,128)}), f32[1024,256]{1,0:T(8,128)}) %all-reduce.9.cloned.1.call-update) | async-done | bytes 1048592 | tf_op jit(solution)/shard_map/psum | solution.py:27
  293.3 3.7 fusion.54
  297.0 27.9 %reduce-scatter.12.cloned.1.call-done = f32[1024,64]{0,1:T(8,128)} async-done(((f32[1024,256]{0,1:T(8,128)}), f32[1024,64]{0,1:T(8,128)}) %reduce-scatter.12.cloned.1.call-update) | async-done | bytes 262160 | tf_op jit(solution)/shard_map/reduce_scatter | solution.py:30
  324.9 1.7 bitcast_dynamic-update-slice_fusion.1
  326.6 0.9 collective-permute-start.6
  327.5 2.5 fusion.6
  330.0 1.6 collective-permute-done.6
  331.6 1.2 collective-permute-start.7
  332.8 2.3 fusion.4
  335.1 9.5 %collective-permute-done.7 = bf16[1024,128]{0,1:T(8,128)(2,1)S(1)} collective-permute-done((bf16[1024,128]{0,1:T(8,128)(2,1)S(1)}, bf16[1024,128]{0,1:T(8,128)(2,1)S(1)}, u32[]{:S(2)}, u32[]{:S(2)}) %collective-permute-start.7) | collective-permute-done | bytes 262176 | tf_op jit(solution)/shard_map/ppermute | solution.py:39
  344.7 3.0 fusion.2
  347.6 3.4 fusion.84
  351.1 36.6 %all-reduce.11.cloned.1.call-done = f32[1024,256]{1,0:T(8,128)} async-done(((f32[1024,256]{1,0:T(8,128)}), f32[1024,256]{1,0:T(8,128)}) %all-reduce.11.cloned.1.call-update) | async-done | bytes 1048592 | tf_op jit(solution)/shard_map/psum | solution.py:27
  387.6 3.7 fusion.57
  391.3 27.9 %reduce-scatter.14.cloned.1.call-done = f32[1024,64]{0,1:T(8,128)} async-done(((f32[1024,256]{0,1:T(8,128)}), f32[1024,64]{0,1:T(8,128)}) %reduce-scatter.14.cloned.1.call-update) | async-done | bytes 262160 | tf_op jit(solution)/shard_map/reduce_scatter | solution.py:30
  419.2 1.6 bitcast_dynamic-update-slice_fusion
  (30 shorter events, 2.2 us)
Async XLA Ops:
  6.5 33.6 %reduce-scatter.6.cloned.1.call-start = ((), (), s32[]{:S(2)}) async-start(), calls=%async_computation.5 | async-start | bytes 1310720 | tf_op jit(solution)/shard_map/reduce_scatter | solution.py:30
  10.0 91.5 %all-reduce.5.cloned.1.call-start = ((), (), s32[]{:S(2)}) async-start(), calls=%async_computation.6 | async-start | bytes 2097152 | tf_op jit(solution)/shard_map/psum | solution.py:27
  41.8 5.0 %collective-permute-start = (bf16[1024,64]{0,1:T(8,128)(2,1)S(1)}, bf16[1024,64]{0,1:T(8,128)(2,1)S(1)}, u32[]{:S(2)}, u32[]{:S(2)}) collective-permute-start(bf16[1024,64]{0,1:T(8,128)(2,1)S(1)} %get-tuple-element.13), channel_id=1, source_target_pairs={{0,12},{4,0},{8,4},{12,8},{1,13},{5,1},{9,5},{13,9},{2,14},{6,2},{... | collective-permute-start | bytes 393224 | tf_op jit(solution)/shard_map/ppermute | solution.py:39
  46.8 13.1 %collective-permute-start.1 = (bf16[1024,128]{0,1:T(8,128)(2,1)S(1)}, bf16[1024,128]{0,1:T(8,128)(2,1)S(1)}, u32[]{:S(2)}, u32[]{:S(2)}) collective-permute-start(bf16[1024,128]{0,1:T(8,128)(2,1)S(1)} %pad_maximum_fusion), channel_id=1, source_target_pairs={{0,8},{4,12},{8,0},{12,4},{1,9},{5,13},{9,1},{13,5},{2,10},{6,14},... | collective-permute-start | bytes 786440 | tf_op jit(solution)/shard_map/ppermute | solution.py:39
  61.3 40.1 %copy-start = (bf16[5,1024,256]{2,1,0:T(8,128)(2,1)S(1)}, bf16[5,1024,256]{2,1,0:T(8,128)(2,1)}, u32[]{:S(2)}) copy-start(bf16[5,1024,256]{2,1,0:T(8,128)(2,1)} %param.7) | copy-start | bytes 7864324
  64.8 68.2 %reduce-scatter.8.cloned.1.call-start = ((), (), s32[]{:S(2)}) async-start(), calls=%async_computation.7 | async-start | bytes 1310720 | tf_op jit(solution)/shard_map/reduce_scatter | solution.py:30
  105.1 92.2 %all-reduce.7.cloned.1.call-start = ((), (), s32[]{:S(2)}) async-start(), calls=%async_computation.8 | async-start | bytes 2097152 | tf_op jit(solution)/shard_map/psum | solution.py:27
  134.7 5.0 %collective-permute-start.2 = (bf16[1024,64]{0,1:T(8,128)(2,1)S(1)}, bf16[1024,64]{0,1:T(8,128)(2,1)S(1)}, u32[]{:S(2)}, u32[]{:S(2)}) collective-permute-start(bf16[1024,64]{0,1:T(8,128)(2,1)S(1)} %get-tuple-element.11), channel_id=1, source_target_pairs={{0,12},{4,0},{8,4},{12,8},{1,13},{5,1},{9,5},{13,9},{2,14},{6,2},{... | collective-permute-start | bytes 393224 | tf_op jit(solution)/shard_map/ppermute | solution.py:39
  139.7 13.1 %collective-permute-start.3 = (bf16[1024,128]{0,1:T(8,128)(2,1)S(1)}, bf16[1024,128]{0,1:T(8,128)(2,1)S(1)}, u32[]{:S(2)}, u32[]{:S(2)}) collective-permute-start(bf16[1024,128]{0,1:T(8,128)(2,1)S(1)} %pad_maximum_fusion.1), channel_id=1, source_target_pairs={{0,8},{4,12},{8,0},{12,4},{1,9},{5,13},{9,1},{13,5},{2,10},{6,14},... | collective-permute-start | bytes 786440 | tf_op jit(solution)/shard_map/ppermute | solution.py:39
  154.2 0.8 copy-start.1
  160.8 68.2 %reduce-scatter.10.cloned.1.call-start = ((), (), s32[]{:S(2)}) async-start(), calls=%async_computation.9 | async-start | bytes 1310720 | tf_op jit(solution)/shard_map/reduce_scatter | solution.py:30
  201.1 92.2 %all-reduce.9.cloned.1.call-start = ((), (), s32[]{:S(2)}) async-start(), calls=%async_computation.10 | async-start | bytes 2097152 | tf_op jit(solution)/shard_map/psum | solution.py:27
  230.6 5.0 %collective-permute-start.4 = (bf16[1024,64]{0,1:T(8,128)(2,1)S(1)}, bf16[1024,64]{0,1:T(8,128)(2,1)S(1)}, u32[]{:S(2)}, u32[]{:S(2)}) collective-permute-start(bf16[1024,64]{0,1:T(8,128)(2,1)S(1)} %get-tuple-element.9), channel_id=1, source_target_pairs={{0,12},{4,0},{8,4},{12,8},{1,13},{5,1},{9,5},{13,9},{2,14},{6,2},{... | collective-permute-start | bytes 393224 | tf_op jit(solution)/shard_map/ppermute | solution.py:39
  235.6 13.1 %collective-permute-start.5 = (bf16[1024,128]{0,1:T(8,128)(2,1)S(1)}, bf16[1024,128]{0,1:T(8,128)(2,1)S(1)}, u32[]{:S(2)}, u32[]{:S(2)}) collective-permute-start(bf16[1024,128]{0,1:T(8,128)(2,1)S(1)} %pad_maximum_fusion.2), channel_id=1, source_target_pairs={{0,8},{4,12},{8,0},{12,4},{1,9},{5,13},{9,1},{13,5},{2,10},{6,14},... | collective-permute-start | bytes 786440 | tf_op jit(solution)/shard_map/ppermute | solution.py:39
  250.2 0.8 copy-start.2
  256.7 68.2 %reduce-scatter.12.cloned.1.call-start = ((), (), s32[]{:S(2)}) async-start(), calls=%async_computation.11 | async-start | bytes 1310720 | tf_op jit(solution)/shard_map/reduce_scatter | solution.py:30
  297.0 90.7 %all-reduce.11.cloned.1.call-start = ((), (), s32[]{:S(2)}) async-start(), calls=%async_computation.12 | async-start | bytes 2097152 | tf_op jit(solution)/shard_map/psum | solution.py:27
  324.9 7.9 %copy-start.3 = (bf16[1024,256]{0,1:T(8,128)(2,1)S(1)}, bf16[1024,256]{0,1:T(8,128)(2,1)}, u32[]{:S(2)}) copy-start(bf16[1024,256]{0,1:T(8,128)(2,1)} %copy-done.2) | copy-start | bytes 1572868
  326.6 5.0 %collective-permute-start.6 = (bf16[1024,64]{0,1:T(8,128)(2,1)S(1)}, bf16[1024,64]{0,1:T(8,128)(2,1)S(1)}, u32[]{:S(2)}, u32[]{:S(2)}) collective-permute-start(bf16[1024,64]{0,1:T(8,128)(2,1)S(1)} %get-tuple-element.7), channel_id=1, source_target_pairs={{0,12},{4,0},{8,4},{12,8},{1,13},{5,1},{9,5},{13,9},{2,14},{6,2},{... | collective-permute-start | bytes 393224 | tf_op jit(solution)/shard_map/ppermute | solution.py:39
  331.6 13.1 %collective-permute-start.7 = (bf16[1024,128]{0,1:T(8,128)(2,1)S(1)}, bf16[1024,128]{0,1:T(8,128)(2,1)S(1)}, u32[]{:S(2)}, u32[]{:S(2)}) collective-permute-start(bf16[1024,128]{0,1:T(8,128)(2,1)S(1)} %pad_maximum_fusion.3), channel_id=1, source_target_pairs={{0,8},{4,12},{8,0},{12,4},{1,9},{5,13},{9,1},{13,5},{2,10},{6,14},... | collective-permute-start | bytes 786440 | tf_op jit(solution)/shard_map/ppermute | solution.py:39
  351.0 68.2 %reduce-scatter.14.cloned.1.call-start = ((), (), s32[]{:S(2)}) async-start(), calls=%async_computation.13 | async-start | bytes 1310720 | tf_op jit(solution)/shard_map/reduce_scatter | solution.py:30
Sparse Core Ops, SparseCore 0:
  10.1 29.9 reduce-scatter.5
  64.9 36.4 all-reduce.4
  105.3 27.7 reduce-scatter.7
  160.9 36.4 all-reduce.6
  201.2 27.7 reduce-scatter.9
  256.8 36.4 all-reduce.8
  297.1 27.7 reduce-scatter.11
  351.1 36.4 all-reduce.10
  391.4 27.7 reduce-scatter.13
